TPU v7x, 32 devices: a whole 2x2x4 slice. The times are simulated.
32 devices in a mesh: outer: 8 (over z, x), inner: 4 (over y, core).
Axes of the slice: x: 2, y: 2, z: 4, core: 2. Of those that a mesh axis runs over, the one named last changes fastest.
Arguments:
- fine_input: bfloat16 [6144, 2048], P(('outer', 'inner')), may hold values from -12 to 12
- fine_query: bfloat16 [6144, 1024], P(('outer', 'inner')), may hold values from -4.5 to 4.5
- fine_key: bfloat16 [6144, 1024], P(('outer', 'inner')), may hold values from -4.5 to 4.5
- fine_value: bfloat16 [6144, 1024], P(('outer', 'inner')), may hold values from -6 to 6
- w_fine_out: bfloat16 [1024, 2048], P(None, 'inner'), may hold values from -0.1875 to 0.1875
- norm_gain: float32 [2048], replicated, may hold values from 0.25 to 1.75
- w_query: bfloat16 [2048, 512], P(None, 'inner'), may hold values from -1 to 1
- w_key: bfloat16 [2048, 512], P(None, 'inner'), may hold values from -1 to 1
- w_value: bfloat16 [2048, 512], P(None, 'inner'), may hold values from -0.125 to 0.125
- w_coarse_out: bfloat16 [512, 2048], P('inner'), may hold values from -0.25 to 0.25
Outputs:
- mixed_stream: bfloat16 [6144, 2048], P(('outer', 'inner'))
All inputs are finite; a program needn't handle non-finite values.
Results may differ from a plain program's by a relative error of at most 0.008.
Values may be sent and summed in bfloat16 or wider, within the bound.
No kernel may reach another device: no remote copies, remote signals or barrier semaphores. Data moves between devices by JAX's collectives and lax.ppermute only.
A program may use at most 128 MiB of HBM per device.

v0:
```python
import math
import jax
import jax.numpy as jnp
from jax import lax
from jax.sharding import PartitionSpec as P

HE = 128
WIN = 512
POOL = 8
very_negative = -1e30


def passed_along(block, axis, distance):
    devices = range(lax.axis_size(axis))
    route = [(i - distance, i) for i in devices if i - distance in devices]
    return lax.ppermute(block, axis, route)


def on_device(
    fine_input,
    fine_query,
    fine_key,
    fine_value,
    w_fine_out,
    norm_gain,
    w_query,
    w_key,
    w_value,
    w_coarse_out,
):
    tok_rows, model_width = fine_input.shape
    fine_heads = fine_query.shape[1] // HE
    score_scale = 1.0 / math.sqrt(HE)
    reach_count = (WIN + tok_rows - 1) // tok_rows
    position = lax.axis_index(("outer", "inner"))
    key_list = []
    value_list = []
    for distance in range(reach_count, 0, -1):
        shifted = passed_along((fine_key, fine_value), ("outer", "inner"), distance)
        key_list.append(shifted[0])
        value_list.append(shifted[1])
    key_list.append(fine_key)
    value_list.append(fine_value)
    span = (reach_count + 1) * tok_rows
    key_heads = jnp.concatenate(key_list, axis=0).reshape(span, fine_heads, HE)
    value_heads = jnp.concatenate(value_list, axis=0).reshape(span, fine_heads, HE)
    query_heads = fine_query.reshape(tok_rows, fine_heads, HE)
    scores = (
        jnp.einsum("qhe,khe->hqk", query_heads, key_heads, preferred_element_type=jnp.float32)
        * score_scale
    )
    row_ids = jnp.arange(tok_rows, dtype=jnp.int32)[:, None] + reach_count * tok_rows
    col_ids = jnp.arange(span, dtype=jnp.int32)[None, :]
    gap_rows = row_ids - col_ids
    allowed = (
        (gap_rows >= 0) & (gap_rows < WIN) & ((position - reach_count) * tok_rows + col_ids >= 0)
    )
    masked = jnp.where(allowed[None], scores, very_negative)
    row_max = jnp.max(masked, axis=-1, keepdims=True)
    exp_weights = jnp.where(allowed[None], jnp.exp(scores - row_max), 0.0)
    row_sum = jnp.sum(exp_weights, axis=-1)
    summed = jnp.einsum(
        "hqk,khe->qhe",
        exp_weights.astype(jnp.bfloat16),
        value_heads,
        preferred_element_type=jnp.float32,
    )
    fine_mix = (
        (summed / jnp.transpose(row_sum)[:, :, None])
        .astype(jnp.bfloat16)
        .reshape(tok_rows, fine_heads * HE)
    )
    projected = jnp.dot(
        fine_mix,
        lax.all_gather(w_fine_out, "inner", axis=1, tiled=True),
        preferred_element_type=jnp.float32,
    )
    fine_state = (fine_input.astype(jnp.float32) + projected).astype(jnp.bfloat16)
    edge_rows = passed_along(fine_state[tok_rows - POOL + 1 :], ("outer", "inner"), 1)
    first_pool = (
        jnp.sum(edge_rows, axis=0, dtype=jnp.float32) + fine_state[0].astype(jnp.float32)
    ) / POOL
    later_pools = (
        jnp.sum(
            fine_state[1 : tok_rows - POOL + 1].reshape(tok_rows // POOL - 1, POOL, model_width),
            axis=1,
            dtype=jnp.float32,
        )
        / POOL
    )
    pooled = jnp.concatenate([first_pool[None], later_pools], axis=0).astype(jnp.bfloat16)
    pooled_wide = pooled.astype(jnp.float32)
    moment = jnp.mean(pooled_wide * pooled_wide, axis=-1, keepdims=True)
    normed = (pooled_wide * lax.rsqrt(moment + 1e-06) * norm_gain).astype(jnp.bfloat16)
    local_heads = w_query.shape[1] // HE
    head_width = local_heads * HE
    joined_weights = jnp.concatenate([w_query, w_key, w_value], axis=1)
    projections = jnp.dot(
        lax.all_gather(normed, "inner", axis=0, tiled=True),
        joined_weights,
        preferred_element_type=jnp.float32,
    ).astype(jnp.bfloat16)
    group_len = projections.shape[0]
    coarse_query = projections[:, :head_width].reshape(group_len, local_heads, HE)
    coarse_key = projections[:, head_width : 2 * head_width]
    coarse_value = projections[:, 2 * head_width :]
    outer_index = lax.axis_index("outer")
    query_pos = outer_index * group_len + jnp.arange(group_len, dtype=jnp.int32)
    pieces = (
        lax.all_gather(coarse_key, "outer", axis=0, tiled=True),
        lax.all_gather(coarse_value, "outer", axis=0, tiled=True),
    )
    prior_max = jnp.full((local_heads, group_len), very_negative, jnp.float32)
    count = pieces[0].shape[0]
    block_keys = pieces[0].reshape(count, local_heads, HE)
    block_values = pieces[1].reshape(count, local_heads, HE)
    block_scores = (
        jnp.einsum("qhe,khe->hqk", coarse_query, block_keys, preferred_element_type=jnp.float32)
        * score_scale
    )
    key_pos = jnp.arange(count, dtype=jnp.int32)
    visible = (key_pos[None, :] <= query_pos[:, None])[None]
    block_masked = jnp.where(visible, block_scores, very_negative)
    new_max = jnp.maximum(prior_max, jnp.max(block_masked, axis=-1))
    block_exp = jnp.where(visible, jnp.exp(block_scores - new_max[:, :, None]), 0.0)
    new_sum = jnp.sum(block_exp, axis=-1)
    contrib = jnp.einsum(
        "hqk,khe->hqe",
        block_exp.astype(jnp.bfloat16),
        block_values,
        preferred_element_type=jnp.float32,
    )
    coarse_mix = (
        jnp.transpose(contrib / new_sum[:, :, None], (1, 0, 2))
        .reshape(group_len, head_width)
        .astype(jnp.bfloat16)
    )
    head_total = lax.psum_scatter(
        jnp.dot(coarse_mix, w_coarse_out, preferred_element_type=jnp.float32).astype(jnp.bfloat16),
        "inner",
        scatter_dimension=0,
        tiled=True,
    ).astype(jnp.float32)
    coarse_out = (pooled_wide + head_total).astype(jnp.bfloat16)
    fine_groups = fine_state.reshape(tok_rows // POOL, POOL, model_width).astype(jnp.float32)
    lifted = fine_groups + coarse_out.astype(jnp.float32)[:, None, :]
    return lifted.reshape(tok_rows, model_width).astype(jnp.bfloat16)


def solution(mesh):
    placed = (
        P(("outer", "inner"), None),
        P(("outer", "inner"), None),
        P(("outer", "inner"), None),
        P(("outer", "inner"), None),
        P(None, "inner"),
        P(),
        P(None, "inner"),
        P(None, "inner"),
        P(None, "inner"),
        P("inner", None),
    )
    return jax.shard_map(
        on_device,
        mesh=mesh,
        in_specs=placed,
        out_specs=P(("outer", "inner"), None),
        check_vma=False,
    )
```

profile of v0, /device:TPU:0, one launch (start us, length us, event | category | flops | bytes accessed | tf_op | source)
XLA Modules:
  0.0 202.3 jit_solution(12393071811701069702)
XLA Ops:
  6.5 0.0 copy-start
  6.5 0.0 all-gather.2.cloned.1.call-start
  6.5 0.7 all-gather.2.cloned.1.call-update
  7.3 0.0 reduce-scatter.2.cloned.1.call-start
  7.3 1.2 copy.16
  8.5 4.4 %collective-permute-start.3 = (bf16[192,1024]{0,1:T(8,128)(2,1)S(1)}, bf16[192,1024]{0,1:T(8,128)(2,1)S(1)}, u32[]{:S(2)}, u32[]{:S(2)}) collective-permute-start(bf16[192,1024]{0,1:T(8,128)(2,1)S(1)} %copy.16), channel_id=1, source_target_pairs={{0,3},{1,4},{2,5},{3,6},{4,7},{5,8},{6,9},{7,10},{8,11},{9,12},{10... | collective-permute-start | bytes 1179656 | tf_op jit(solution)/shard_map/ppermute | solution.py:16
  12.9 3.4 %collective-permute-start.4 = (bf16[192,1024]{0,1:T(8,128)(2,1)S(1)}, bf16[192,1024]{0,1:T(8,128)(2,1)S(1)}, u32[]{:S(2)}, u32[]{:S(2)}) collective-permute-start(bf16[192,1024]{0,1:T(8,128)(2,1)S(1)} %copy.16), channel_id=1, source_target_pairs={{0,2},{1,3},{2,4},{3,5},{4,6},{5,7},{6,8},{7,9},{8,10},{9,11},{10,... | collective-permute-start | bytes 1179656 | tf_op jit(solution)/shard_map/ppermute | solution.py:16
  16.3 3.1 %collective-permute-start.5 = (bf16[192,1024]{0,1:T(8,128)(2,1)S(1)}, bf16[192,1024]{0,1:T(8,128)(2,1)}, u32[]{:S(2)}, u32[]{:S(2)}) collective-permute-start(bf16[192,1024]{0,1:T(8,128)(2,1)S(1)} %copy.16), channel_id=1, source_target_pairs={{0,1},{1,2},{2,3},{3,4},{4,5},{5,6},{6,7},{7,8},{8,9},{9,10},{10,1... | collective-permute-start | bytes 1179656 | tf_op jit(solution)/shard_map/ppermute | solution.py:16
  19.4 1.2 copy.12
  20.6 4.2 %collective-permute-start = (bf16[192,1024]{0,1:T(8,128)(2,1)S(1)}, bf16[192,1024]{0,1:T(8,128)(2,1)}, u32[]{:S(2)}, u32[]{:S(2)}) collective-permute-start(bf16[192,1024]{0,1:T(8,128)(2,1)S(1)} %copy.12), channel_id=1, source_target_pairs={{0,3},{1,4},{2,5},{3,6},{4,7},{5,8},{6,9},{7,10},{8,11},{9,12},{10... | collective-permute-start | bytes 1179656 | tf_op jit(solution)/shard_map/ppermute | solution.py:16
  24.8 4.2 %collective-permute-start.1 = (bf16[192,1024]{0,1:T(8,128)(2,1)S(1)}, bf16[192,1024]{0,1:T(8,128)(2,1)}, u32[]{:S(2)}, u32[]{:S(2)}) collective-permute-start(bf16[192,1024]{0,1:T(8,128)(2,1)S(1)} %copy.12), channel_id=1, source_target_pairs={{0,2},{1,3},{2,4},{3,5},{4,6},{5,7},{6,8},{7,9},{8,10},{9,11},{10,... | collective-permute-start | bytes 1179656 | tf_op jit(solution)/shard_map/ppermute | solution.py:16
  29.1 0.0 collective-permute-done.3
  29.1 0.0 copy-start.2
  29.1 1.3 collective-permute-start.2
  30.4 0.2 fusion.37
  30.6 16.0 %collective-permute-done.4 = bf16[192,1024]{0,1:T(8,128)(2,1)S(1)} collective-permute-done((bf16[192,1024]{0,1:T(8,128)(2,1)S(1)}, bf16[192,1024]{0,1:T(8,128)(2,1)S(1)}, u32[]{:S(2)}, u32[]{:S(2)}) %collective-permute-start.4) | collective-permute-done | bytes 393248 | tf_op jit(solution)/shard_map/ppermute | solution.py:16
  46.7 0.0 copy-done.2
  46.7 0.0 copy-start.3
  46.7 0.8 copy-done.3
  47.4 0.0 collective-permute-done.5
  47.5 2.1 %pad_maximum_fusion.1 = bf16[768,1024]{0,1:T(8,128)(2,1)S(1)} fusion(bf16[192,1024]{0,1:T(8,128)(2,1)S(1)} %copy.16, bf16[192,1024]{0,1:T(8,128)(2,1)} %collective-permute-done.5, bf16[192,1024]{0,1:T(8,128)(2,1)} %copy-done.3, bf16[192,1024]{0,1:T(8,128)(2,1)} %copy-done.2), kind=kLoop, calls=%fused_computation.16 | loop fusion | flops 6291456 | bytes 3145728 | tf_op jit(solution)/shard_map/concatenate | solution.py:45
  49.6 0.0 copy-start.8
  49.6 17.4 %collective-permute-done = bf16[192,1024]{0,1:T(8,128)(2,1)} collective-permute-done((bf16[192,1024]{0,1:T(8,128)(2,1)S(1)}, bf16[192,1024]{0,1:T(8,128)(2,1)}, u32[]{:S(2)}, u32[]{:S(2)}) %collective-permute-start) | collective-permute-done | bytes 393248 | tf_op jit(solution)/shard_map/ppermute | solution.py:16
  67.0 11.2 %collective-permute-done.1 = bf16[192,1024]{0,1:T(8,128)(2,1)} collective-permute-done((bf16[192,1024]{0,1:T(8,128)(2,1)S(1)}, bf16[192,1024]{0,1:T(8,128)(2,1)}, u32[]{:S(2)}, u32[]{:S(2)}) %collective-permute-start.1) | collective-permute-done | bytes 393248 | tf_op jit(solution)/shard_map/ppermute | solution.py:16
  78.2 0.0 collective-permute-done.2
  78.2 3.1 %pad_maximum_fusion = bf16[768,1024]{0,1:T(8,128)(2,1)} fusion(bf16[192,1024]{0,1:T(8,128)(2,1)S(1)} %copy.12, bf16[192,1024]{0,1:T(8,128)(2,1)S(1)} %collective-permute-done.2, bf16[192,1024]{0,1:T(8,128)(2,1)} %collective-permute-done.1, bf16[192,1024]{0,1:T(8,128)(2,1)} %collective-permute-done), kind=kLoop, calls=%fused_computation.15 | loop fusion | flops 6291456 | bytes 3145728 | tf_op jit(solution)/shard_map/concatenate | solution.py:46
  81.3 0.0 copy-done.8
  81.3 3.7 %fusion.79 = (f32[8,192]{1,0:T(8,128)S(1)}, bf16[8,192,768]{2,1,0:T(8,128)(2,1)}) fusion(pred[192,768]{1,0:T(8,128)(4,1)S(1)} %fusion.37, bf16[768,8,128]{0,2,1:T(8,128)(2,1)S(1)} %bitcast.70, bf16[192,1024]{1,0:T(8,128)(2,1)S(1)} %copy-done.8), kind=kOutput, calls=%fused_computation.83 | convolution fusion | flops 612238080 | bytes 4478976 | tf_op jit(solution)/shard_map/sub | solution.py:60
  85.0 0.0 copy-start.1
  85.0 3.0 %fusion.27 = bf16[8,24,8,128]{3,2,1,0:T(8,128)(2,1)S(1)} fusion(bf16[768,8,128]{0,2,1:T(8,128)(2,1)} %bitcast.71, bf16[8,192,768]{2,1,0:T(8,128)(2,1)} %get-tuple-element.8, f32[192,8]{0,1:T(8,128)S(1)} %bitcast.73), kind=kOutput, calls=%fused_computation.29 | convolution fusion | flops 302383104 | bytes 4331520 | tf_op jit(solution)/shard_map/hqk,khe->qhe/dot_general | solution.py:62
  88.0 0.0 copy-start.4
  88.0 0.0 copy-start.5
  88.0 0.0 all-gather.2.cloned.1.call-done
  88.1 0.0 copy-done.1
  88.1 0.0 copy-start.6
  88.1 0.0 copy-start.7
  88.1 3.3 %fusion.5 = bf16[192,2048]{1,0:T(8,128)(2,1)S(1)} fusion(bf16[1024,2048]{1,0:T(8,128)(2,1)} %all-gather.2.cloned.1.call-done, bf16[192,2048]{1,0:T(8,128)(2,1)S(1)} %copy-done.1, bf16[8,24,8,128]{3,2,1,0:T(8,128)(2,1)S(1)} %fusion.27), kind=kOutput, calls=%fused_computation.8 | convolution fusion | flops 806486016 | bytes 6160384 | tf_op jit(solution)/shard_map/dot_general | solution.py:73
  91.4 0.5 convert_reduce_fusion
  92.0 5.1 %collective-permute-start.6 = (bf16[7,2048]{1,0:T(8,128)(2,1)S(1)}, bf16[7,2048]{1,0:T(8,128)(2,1)S(1)}, u32[]{:S(2)}, u32[]{:S(2)}) collective-permute-start(bf16[7,2048]{1,0:T(8,128)(2,1)S(1)} %slice.24), channel_id=1, source_target_pairs={{0,1},{1,2},{2,3},{3,4},{4,5},{5,6},{6,7},{7,8},{8,9},{9,10},{10,1... | collective-permute-start | bytes 86024 | tf_op jit(solution)/shard_map/ppermute | solution.py:16
  97.1 0.8 collective-permute-done.6
  98.0 0.2 fusion.55
  98.2 0.0 copy-done.4
  98.2 0.1 fusion.57
  98.3 9.8 %all_gather.13 = bf16[96,2048]{1,0:T(8,128)(2,1)S(1)} all-gather(bf16[24,2048]{1,0:T(8,128)(2,1)S(1)} %fusion.57), channel_id=1, replica_groups=mesh['outer'=8,'inner'=4] {'inner'}, dimensions={0}, use_global_device_ids=true | all-gather | bytes 491520 | tf_op jit(solution)/shard_map/all_gather | solution.py:99
  108.1 0.0 copy-done.5
  108.1 0.0 copy-done.6
  108.1 0.0 copy-done.7
  108.1 0.4 fusion.30
  108.5 31.0 %all_gather.14 = bf16[768,128]{1,0:T(8,128)(2,1)S(1)} all-gather(bf16[96,128]{1,0:T(8,128)(2,1)S(1)} %get-tuple-element.5), channel_id=1, replica_groups=mesh['outer'=8,'inner'=4] {'outer'}, dimensions={0}, use_global_device_ids=true | all-gather | bytes 221184 | tf_op jit(solution)/shard_map/all_gather | solution.py:110
  139.5 0.3 select_reduce_fusion
  139.9 30.6 %all_gather.15 = bf16[768,128]{1,0:T(8,128)(2,1)S(1)} all-gather(bf16[96,128]{1,0:T(8,128)(2,1)S(1)} %get-tuple-element.6), channel_id=1, replica_groups=mesh['outer'=8,'inner'=4] {'outer'}, dimensions={0}, use_global_device_ids=true | all-gather | bytes 221184 | tf_op jit(solution)/shard_map/all_gather | solution.py:111
  170.5 0.2 fusion.53
  170.7 0.0 copy-done
  170.7 1.2 convolution_convert_fusion
  171.9 0.0 reduce-scatter.2.cloned.1.call-update
  172.0 21.5 %reduce-scatter.2.cloned.1.call-done = bf16[24,2048]{1,0:T(8,128)(2,1)} async-done(((bf16[96,2048]{1,0:T(8,128)(2,1)}), bf16[24,2048]{1,0:T(8,128)(2,1)}) %reduce-scatter.2.cloned.1.call-update) | async-done | bytes 98320 | tf_op jit(solution)/shard_map/reduce_scatter | solution.py:138
  193.4 0.9 fusion.67
  194.4 1.1 fusion.17
  (10 shorter events, 0.1 us)
Async XLA Ops:
  6.5 164.2 %copy-start = (bf16[128,2048]{1,0:T(8,128)(2,1)S(1)}, bf16[128,2048]{1,0:T(8,128)(2,1)}, u32[]{:S(2)}) copy-start(bf16[128,2048]{1,0:T(8,128)(2,1)} %param.19) | copy-start | bytes 1572868
  6.5 81.5 %all-gather.2.cloned.1.call-start = ((), (), s32[]{:S(2)}) async-start(), calls=%async_computation.1 | async-start | bytes 5242880 | tf_op jit(solution)/shard_map/all_gather | solution.py:75
  7.3 186.2 %reduce-scatter.2.cloned.1.call-start = ((), (), s32[]{:S(2)}) async-start(), calls=%async_computation.2 | async-start | bytes 491520 | tf_op jit(solution)/shard_map/reduce_scatter | solution.py:138
  8.5 20.6 %collective-permute-start.3 = (bf16[192,1024]{0,1:T(8,128)(2,1)S(1)}, bf16[192,1024]{0,1:T(8,128)(2,1)S(1)}, u32[]{:S(2)}, u32[]{:S(2)}) collective-permute-start(bf16[192,1024]{0,1:T(8,128)(2,1)S(1)} %copy.16), channel_id=1, source_target_pairs={{0,3},{1,4},{2,5},{3,6},{4,7},{5,8},{6,9},{7,10},{8,11},{9,12},{10... | collective-permute-start | bytes 1179656 | tf_op jit(solution)/shard_map/ppermute | solution.py:16
  12.9 33.8 %collective-permute-start.4 = (bf16[192,1024]{0,1:T(8,128)(2,1)S(1)}, bf16[192,1024]{0,1:T(8,128)(2,1)S(1)}, u32[]{:S(2)}, u32[]{:S(2)}) collective-permute-start(bf16[192,1024]{0,1:T(8,128)(2,1)S(1)} %copy.16), channel_id=1, source_target_pairs={{0,2},{1,3},{2,4},{3,5},{4,6},{5,7},{6,8},{7,9},{8,10},{9,11},{10,... | collective-permute-start | bytes 1179656 | tf_op jit(solution)/shard_map/ppermute | solution.py:16
  16.3 31.2 %collective-permute-start.5 = (bf16[192,1024]{0,1:T(8,128)(2,1)S(1)}, bf16[192,1024]{0,1:T(8,128)(2,1)}, u32[]{:S(2)}, u32[]{:S(2)}) collective-permute-start(bf16[192,1024]{0,1:T(8,128)(2,1)S(1)} %copy.16), channel_id=1, source_target_pairs={{0,1},{1,2},{2,3},{3,4},{4,5},{5,6},{6,7},{7,8},{8,9},{9,10},{10,1... | collective-permute-start | bytes 1179656 | tf_op jit(solution)/shard_map/ppermute | solution.py:16
  20.6 46.3 %collective-permute-start = (bf16[192,1024]{0,1:T(8,128)(2,1)S(1)}, bf16[192,1024]{0,1:T(8,128)(2,1)}, u32[]{:S(2)}, u32[]{:S(2)}) collective-permute-start(bf16[192,1024]{0,1:T(8,128)(2,1)S(1)} %copy.12), channel_id=1, source_target_pairs={{0,3},{1,4},{2,5},{3,6},{4,7},{5,8},{6,9},{7,10},{8,11},{9,12},{10... | collective-permute-start | bytes 1179656 | tf_op jit(solution)/shard_map/ppermute | solution.py:16
  24.8 53.4 %collective-permute-start.1 = (bf16[192,1024]{0,1:T(8,128)(2,1)S(1)}, bf16[192,1024]{0,1:T(8,128)(2,1)}, u32[]{:S(2)}, u32[]{:S(2)}) collective-permute-start(bf16[192,1024]{0,1:T(8,128)(2,1)S(1)} %copy.12), channel_id=1, source_target_pairs={{0,2},{1,3},{2,4},{3,5},{4,6},{5,7},{6,8},{7,9},{8,10},{9,11},{10,... | collective-permute-start | bytes 1179656 | tf_op jit(solution)/shard_map/ppermute | solution.py:16
  29.1 17.6 %copy-start.2 = (bf16[192,1024]{0,1:T(8,128)(2,1)}, bf16[192,1024]{0,1:T(8,128)(2,1)S(1)}, u32[]{:S(2)}) copy-start(bf16[192,1024]{0,1:T(8,128)(2,1)S(1)} %collective-permute-done.3) | copy-start | bytes 1179652
  29.1 49.1 %collective-permute-start.2 = (bf16[192,1024]{0,1:T(8,128)(2,1)S(1)}, bf16[192,1024]{0,1:T(8,128)(2,1)S(1)}, u32[]{:S(2)}, u32[]{:S(2)}) collective-permute-start(bf16[192,1024]{0,1:T(8,128)(2,1)S(1)} %copy.12), channel_id=1, source_target_pairs={{0,1},{1,2},{2,3},{3,4},{4,5},{5,6},{6,7},{7,8},{8,9},{9,10},{10,1... | collective-permute-start | bytes 1179656 | tf_op jit(solution)/shard_map/ppermute | solution.py:16
  46.7 0.8 copy-start.3
  49.6 31.8 %copy-start.8 = (bf16[192,1024]{1,0:T(8,128)(2,1)S(1)}, bf16[192,1024]{1,0:T(8,128)(2,1)}, u32[]{:S(2)}) copy-start(bf16[192,1024]{1,0:T(8,128)(2,1)} %param.11) | copy-start | bytes 1179652
  85.0 3.0 %copy-start.1 = (bf16[192,2048]{1,0:T(8,128)(2,1)S(1)}, bf16[192,2048]{1,0:T(8,128)(2,1)}, u32[]{:S(2)}) copy-start(bf16[192,2048]{1,0:T(8,128)(2,1)} %param.10) | copy-start | bytes 2359300
  88.0 10.1 %copy-start.4 = (f32[2048]{0:T(1024)S(1)}, f32[2048]{0:T(1024)}, u32[]{:S(2)}) copy-start(f32[2048]{0:T(1024)} %param.15) | copy-start | bytes 24580
  88.0 20.0 %copy-start.5 = (bf16[2048,128]{1,0:T(8,128)(2,1)S(1)}, bf16[2048,128]{1,0:T(8,128)(2,1)}, u32[]{:S(2)}) copy-start(bf16[2048,128]{1,0:T(8,128)(2,1)} %param.18) | copy-start | bytes 1572868
  88.1 20.0 %copy-start.6 = (bf16[2048,128]{1,0:T(8,128)(2,1)S(1)}, bf16[2048,128]{1,0:T(8,128)(2,1)}, u32[]{:S(2)}) copy-start(bf16[2048,128]{1,0:T(8,128)(2,1)} %param.17) | copy-start | bytes 1572868
  88.1 20.0 %copy-start.7 = (bf16[2048,128]{1,0:T(8,128)(2,1)S(1)}, bf16[2048,128]{1,0:T(8,128)(2,1)}, u32[]{:S(2)}) copy-start(bf16[2048,128]{1,0:T(8,128)(2,1)} %param.16) | copy-start | bytes 1572868
  92.0 6.0 %collective-permute-start.6 = (bf16[7,2048]{1,0:T(8,128)(2,1)S(1)}, bf16[7,2048]{1,0:T(8,128)(2,1)S(1)}, u32[]{:S(2)}, u32[]{:S(2)}) collective-permute-start(bf16[7,2048]{1,0:T(8,128)(2,1)S(1)} %slice.24), channel_id=1, source_target_pairs={{0,1},{1,2},{2,3},{3,4},{4,5},{5,6},{6,7},{7,8},{8,9},{9,10},{10,1... | collective-permute-start | bytes 86024 | tf_op jit(solution)/shard_map/ppermute | solution.py:16
Sparse Core Ops, SparseCore 0:
  8.9 56.0 all-gather.1
  172.1 21.3 reduce-scatter.1
where the time goes:
time: 203 us; the launch traced here: 202 us
  blocking collectives  71.5 us (35%)
  waiting for transfers between devices  67.7 us (33%)
  starting transfers between devices  25.8 us (13%)
  between operations  13.6 us (7%)
  matrix products  11.9 us (6%)
  other arithmetic  8.52 us (4%)
  local copies, waits for them, and re-layouts  3.27 us (2%)
    ppermute x7, waiting for transfers between devices, passed_along(): return lax.ppermute(block, axis, route)  45.5 us
    all_gather x1, blocking collectives, on_device(): lax.all_gather(coarse_key, 'outer', axis=0, tiled=True)  31 us
    all_gather x1, blocking collectives, on_device(): lax.all_gather(coarse_value, 'outer', axis=0, tiled=True)  30.6 us
    ppermute x7, starting transfers between devices, passed_along(): return lax.ppermute(block, axis, route)  25.7 us
    reduce_scatter x1, waiting for transfers between devices, on_device(): lax.psum_scatter(jnp.dot(coarse_mix, w_coarse_out, preferred_element_type...  21.5 us
    all_gather x1, blocking collectives, on_device(): lax.all_gather(normed, 'inner', axis=0, tiled=True)  9.81 us
  transfers between devices with their start and end apart: 9, of which 5 were waited for; matrix products, arithmetic and copies ran while one was open for 7% of the time, Pallas kernels for 0%

commit v1 on v0

--- a/solution.py
+++ b/solution.py
@@ -8,6 +8,25 @@
 WIN = 512
 POOL = 8
 very_negative = -1e30
+
+
+def gather_around(x, axis, dim):
+    size, here, span = (lax.axis_size(axis), lax.axis_index(axis), x.shape[dim])
+    right = [(i, (i + 1) % size) for i in range(size)]
+    left = [(i, (i - 1) % size) for i in range(size)]
+    out = jnp.zeros((*x.shape[:dim], size * span, *x.shape[dim + 1 :]), x.dtype)
+    out = lax.dynamic_update_slice_in_dim(out, x, here * span, axis=dim)
+    from_left = from_right = x
+    halfway = size // 2
+    for hop in range(1, halfway + 1):
+        from_left = lax.ppermute(from_left, axis, right)
+        out = lax.dynamic_update_slice_in_dim(out, from_left, (here - hop) % size * span, axis=dim)
+        if hop < size - halfway:
+            from_right = lax.ppermute(from_right, axis, left)
+            out = lax.dynamic_update_slice_in_dim(
+                out, from_right, (here + hop) % size * span, axis=dim
+            )
+    return out
 
 
 def passed_along(block, axis, distance):
@@ -107,7 +126,7 @@
     outer_index = lax.axis_index("outer")
     query_pos = outer_index * group_len + jnp.arange(group_len, dtype=jnp.int32)
     pieces = (
-        lax.all_gather(coarse_key, "outer", axis=0, tiled=True),
+        gather_around(coarse_key, "outer", 0),
         lax.all_gather(coarse_value, "outer", axis=0, tiled=True),
     )
     prior_max = jnp.full((local_heads, group_len), very_negative, jnp.float32)

time: 203 us -> 193 us (0.951)
  blocking collectives: 71.5 us -> 40.6 us
  starting transfers between devices: 25.8 us -> 40.7 us
  waiting for transfers between devices: 67.7 us -> 74.2 us
    all_gather x1 -> x0, blocking collectives: 31 us -> none  [on_device(): lax.all_gather(coarse_key, 'outer', axis=0, tiled=True)]
    ppermute x0 -> x7, starting transfers between devices: none -> 14.2 us  [the longest x3 12.7 us: gather_around(): from_right = lax.ppermute(from_right, axis, left)]
    ppermute x0 -> x7, waiting for transfers between devices: none -> 10.1 us  [the longest x4 10 us: gather_around(): from_left = lax.ppermute(from_left, axis, right)]
    reduce_scatter x1, waiting for transfers between devices: 21.5 us -> 17.9 us  [on_device(): lax.psum_scatter(jnp.dot(coarse_mix, w_coarse_out, preferred_element_type...]
  transfers between devices with their start and end apart: 9 -> 16, of which waited for: 5 -> 8; matrix products, arithmetic and copies ran while one was open for 7% -> 8% of each run, Pallas kernels for 0% -> 0%
where the time goes in v1:
time: 193 us; the launch traced here: 192 us
  waiting for transfers between devices  74.2 us (38%)
  starting transfers between devices  40.7 us (21%)
  blocking collectives  40.6 us (21%)
  between operations  13.6 us (7%)
  matrix products  11.9 us (6%)
  other arithmetic  8.67 us (4%)
  local copies, waits for them, and re-layouts  2.66 us (1%)
    ppermute x7, waiting for transfers between devices, passed_along(): return lax.ppermute(block, axis, route)  45.5 us
    all_gather x1, blocking collectives, on_device(): lax.all_gather(coarse_value, 'outer', axis=0, tiled=True)  30.6 us
    ppermute x7, starting transfers between devices, passed_along(): return lax.ppermute(block, axis, route)  26.5 us
    reduce_scatter x1, waiting for transfers between devices, on_device(): lax.psum_scatter(jnp.dot(coarse_mix, w_coarse_out, preferred_element_type...  17.9 us
    ppermute x3, starting transfers between devices, gather_around(): from_right = lax.ppermute(from_right, axis, left)  12.7 us
    ppermute x4, waiting for transfers between devices, gather_around(): from_left = lax.ppermute(from_left, axis, right)  10 us
    all_gather x1, blocking collectives, on_device(): lax.all_gather(normed, 'inner', axis=0, tiled=True)  9.93 us
  transfers between devices with their start and end apart: 16, of which 8 were waited for; matrix products, arithmetic and copies ran while one was open for 8% of the time, Pallas kernels for 0%

profile of v1, /device:TPU:0, one launch (start us, length us, event | category | flops | bytes accessed | tf_op | source)
XLA Modules:
  0.0 192.4 jit_solution(14415354243574767826)
XLA Ops:
  6.5 0.0 copy-start
  6.5 0.0 all-gather.2.cloned.1.call-start
  6.5 0.7 all-gather.2.cloned.1.call-update
  7.3 0.0 reduce-scatter.2.cloned.1.call-start
  7.3 1.2 copy.16
  8.5 4.4 %collective-permute-start.3 = (bf16[192,1024]{0,1:T(8,128)(2,1)S(1)}, bf16[192,1024]{0,1:T(8,128)(2,1)S(1)}, u32[]{:S(2)}, u32[]{:S(2)}) collective-permute-start(bf16[192,1024]{0,1:T(8,128)(2,1)S(1)} %copy.16), channel_id=1, source_target_pairs={{0,3},{1,4},{2,5},{3,6},{4,7},{5,8},{6,9},{7,10},{8,11},{9,12},{10... | collective-permute-start | bytes 1179656 | tf_op jit(solution)/shard_map/ppermute | solution.py:35
  12.9 4.2 %collective-permute-start.4 = (bf16[192,1024]{0,1:T(8,128)(2,1)S(1)}, bf16[192,1024]{0,1:T(8,128)(2,1)}, u32[]{:S(2)}, u32[]{:S(2)}) collective-permute-start(bf16[192,1024]{0,1:T(8,128)(2,1)S(1)} %copy.16), channel_id=1, source_target_pairs={{0,2},{1,3},{2,4},{3,5},{4,6},{5,7},{6,8},{7,9},{8,10},{9,11},{10,... | collective-permute-start | bytes 1179656 | tf_op jit(solution)/shard_map/ppermute | solution.py:35
  17.0 3.1 %collective-permute-start.5 = (bf16[192,1024]{0,1:T(8,128)(2,1)S(1)}, bf16[192,1024]{0,1:T(8,128)(2,1)}, u32[]{:S(2)}, u32[]{:S(2)}) collective-permute-start(bf16[192,1024]{0,1:T(8,128)(2,1)S(1)} %copy.16), channel_id=1, source_target_pairs={{0,1},{1,2},{2,3},{3,4},{4,5},{5,6},{6,7},{7,8},{8,9},{9,10},{10,1... | collective-permute-start | bytes 1179656 | tf_op jit(solution)/shard_map/ppermute | solution.py:35
  20.2 1.3 copy.12
  21.5 3.4 %collective-permute-start = (bf16[192,1024]{0,1:T(8,128)(2,1)S(1)}, bf16[192,1024]{0,1:T(8,128)(2,1)}, u32[]{:S(2)}, u32[]{:S(2)}) collective-permute-start(bf16[192,1024]{0,1:T(8,128)(2,1)S(1)} %copy.12), channel_id=1, source_target_pairs={{0,3},{1,4},{2,5},{3,6},{4,7},{5,8},{6,9},{7,10},{8,11},{9,12},{10... | collective-permute-start | bytes 1179656 | tf_op jit(solution)/shard_map/ppermute | solution.py:35
  24.8 4.2 %collective-permute-start.1 = (bf16[192,1024]{0,1:T(8,128)(2,1)S(1)}, bf16[192,1024]{0,1:T(8,128)(2,1)}, u32[]{:S(2)}, u32[]{:S(2)}) collective-permute-start(bf16[192,1024]{0,1:T(8,128)(2,1)S(1)} %copy.12), channel_id=1, source_target_pairs={{0,2},{1,3},{2,4},{3,5},{4,6},{5,7},{6,8},{7,9},{8,10},{9,11},{10,... | collective-permute-start | bytes 1179656 | tf_op jit(solution)/shard_map/ppermute | solution.py:35
  29.1 0.0 collective-permute-done.3
  29.1 0.0 copy-start.2
  29.1 2.1 %collective-permute-start.2 = (bf16[192,1024]{0,1:T(8,128)(2,1)S(1)}, bf16[192,1024]{0,1:T(8,128)(2,1)}, u32[]{:S(2)}, u32[]{:S(2)}) collective-permute-start(bf16[192,1024]{0,1:T(8,128)(2,1)S(1)} %copy.12), channel_id=1, source_target_pairs={{0,1},{1,2},{2,3},{3,4},{4,5},{5,6},{6,7},{7,8},{8,9},{9,10},{10,1... | collective-permute-start | bytes 1179656 | tf_op jit(solution)/shard_map/ppermute | solution.py:35
  31.2 0.2 fusion.37
  31.4 15.2 %collective-permute-done.4 = bf16[192,1024]{0,1:T(8,128)(2,1)} collective-permute-done((bf16[192,1024]{0,1:T(8,128)(2,1)S(1)}, bf16[192,1024]{0,1:T(8,128)(2,1)}, u32[]{:S(2)}, u32[]{:S(2)}) %collective-permute-start.4) | collective-permute-done | bytes 393248 | tf_op jit(solution)/shard_map/ppermute | solution.py:35
  46.7 0.0 copy-done.2
  46.7 0.0 collective-permute-done.5
  46.7 2.1 %pad_maximum_fusion.1 = bf16[768,1024]{0,1:T(8,128)(2,1)S(1)} fusion(bf16[192,1024]{0,1:T(8,128)(2,1)S(1)} %copy.16, bf16[192,1024]{0,1:T(8,128)(2,1)} %collective-permute-done.5, bf16[192,1024]{0,1:T(8,128)(2,1)} %collective-permute-done.4, bf16[192,1024]{0,1:T(8,128)(2,1)} %copy-done.2), kind=kLoop, calls=%fused_computation.16 | loop fusion | flops 6291456 | bytes 3145728 | tf_op jit(solution)/shard_map/concatenate | solution.py:64
  48.8 0.0 copy-start.7
  48.8 18.2 %collective-permute-done = bf16[192,1024]{0,1:T(8,128)(2,1)} collective-permute-done((bf16[192,1024]{0,1:T(8,128)(2,1)S(1)}, bf16[192,1024]{0,1:T(8,128)(2,1)}, u32[]{:S(2)}, u32[]{:S(2)}) %collective-permute-start) | collective-permute-done | bytes 393248 | tf_op jit(solution)/shard_map/ppermute | solution.py:35
  67.0 11.2 %collective-permute-done.1 = bf16[192,1024]{0,1:T(8,128)(2,1)} collective-permute-done((bf16[192,1024]{0,1:T(8,128)(2,1)S(1)}, bf16[192,1024]{0,1:T(8,128)(2,1)}, u32[]{:S(2)}, u32[]{:S(2)}) %collective-permute-start.1) | collective-permute-done | bytes 393248 | tf_op jit(solution)/shard_map/ppermute | solution.py:35
  78.2 0.0 collective-permute-done.2
  78.2 3.2 %pad_maximum_fusion = bf16[768,1024]{0,1:T(8,128)(2,1)} fusion(bf16[192,1024]{0,1:T(8,128)(2,1)S(1)} %copy.12, bf16[192,1024]{0,1:T(8,128)(2,1)} %collective-permute-done.2, bf16[192,1024]{0,1:T(8,128)(2,1)} %collective-permute-done.1, bf16[192,1024]{0,1:T(8,128)(2,1)} %collective-permute-done), kind=kLoop, calls=%fused_computation.15 | loop fusion | flops 6291456 | bytes 3145728 | tf_op jit(solution)/shard_map/concatenate | solution.py:65
  81.5 3.7 %fusion.79 = (f32[8,192]{1,0:T(8,128)S(1)}, bf16[8,192,768]{2,1,0:T(8,128)(2,1)}) fusion(pred[192,768]{1,0:T(8,128)(4,1)S(1)} %fusion.37, bf16[768,8,128]{0,2,1:T(8,128)(2,1)S(1)} %bitcast.70, bf16[192,1024]{1,0:T(8,128)(2,1)S(1)} %copy-done.7), kind=kOutput, calls=%fused_computation.91 | convolution fusion | flops 612238080 | bytes 4478976 | tf_op jit(solution)/shard_map/sub | solution.py:79
  85.2 3.0 %fusion.27 = bf16[8,24,8,128]{3,2,1,0:T(8,128)(2,1)S(1)} fusion(bf16[768,8,128]{0,2,1:T(8,128)(2,1)} %bitcast.71, bf16[8,192,768]{2,1,0:T(8,128)(2,1)} %get-tuple-element.9, f32[192,8]{0,1:T(8,128)S(1)} %bitcast.73), kind=kOutput, calls=%fused_computation.29 | convolution fusion | flops 302383104 | bytes 4331520 | tf_op jit(solution)/shard_map/hqk,khe->qhe/dot_general | solution.py:81
  88.2 0.0 copy-start.3
  88.2 0.0 copy-start.4
  88.2 0.0 all-gather.2.cloned.1.call-done
  88.2 0.0 copy-start.5
  88.2 0.0 copy-start.6
  88.2 3.3 %fusion.5 = bf16[192,2048]{1,0:T(8,128)(2,1)S(1)} fusion(bf16[1024,2048]{1,0:T(8,128)(2,1)} %all-gather.2.cloned.1.call-done, bf16[192,2048]{1,0:T(8,128)(2,1)S(1)} %copy-done.1, bf16[8,24,8,128]{3,2,1,0:T(8,128)(2,1)S(1)} %fusion.27), kind=kOutput, calls=%fused_computation.8 | convolution fusion | flops 806486016 | bytes 6160384 | tf_op jit(solution)/shard_map/dot_general | solution.py:92
  91.5 0.5 convert_reduce_fusion
  92.1 5.1 %collective-permute-start.6 = (bf16[7,2048]{1,0:T(8,128)(2,1)S(1)}, bf16[7,2048]{1,0:T(8,128)(2,1)S(1)}, u32[]{:S(2)}, u32[]{:S(2)}) collective-permute-start(bf16[7,2048]{1,0:T(8,128)(2,1)S(1)} %slice.24), channel_id=1, source_target_pairs={{0,1},{1,2},{2,3},{3,4},{4,5},{5,6},{6,7},{7,8},{8,9},{9,10},{10,1... | collective-permute-start | bytes 86024 | tf_op jit(solution)/shard_map/ppermute | solution.py:35
  97.3 0.8 collective-permute-done.6
  98.1 0.2 fusion.55
  98.3 0.0 copy-done.3
  98.3 0.1 fusion.57
  98.4 9.9 %all_gather.10 = bf16[96,2048]{1,0:T(8,128)(2,1)S(1)} all-gather(bf16[24,2048]{1,0:T(8,128)(2,1)S(1)} %fusion.57), channel_id=1, replica_groups=mesh['outer'=8,'inner'=4] {'inner'}, dimensions={0}, use_global_device_ids=true | all-gather | bytes 491520 | tf_op jit(solution)/shard_map/all_gather | solution.py:118
  108.3 0.0 copy-done.4
  108.3 0.0 copy-done.6
  108.3 0.4 fusion.30
  108.8 1.5 collective-permute-start.7
  110.4 3.2 %collective-permute-start.8 = (bf16[96,128]{1,0:T(8,128)(2,1)S(1)}, bf16[96,128]{1,0:T(8,128)(2,1)S(1)}, u32[]{:S(2)}, u32[]{:S(2)}) collective-permute-start(bf16[96,128]{1,0:T(8,128)(2,1)S(1)} %get-tuple-element.5), channel_id=1, source_target_pairs={{0,28},{4,0},{8,4},{12,8},{16,12},{20,16},{24,20},{28,24},{1,29},{... | collective-permute-start | bytes 73736 | tf_op jit(solution)/shard_map/ppermute | solution.py:25
  113.6 30.6 %all_gather.11 = bf16[768,128]{1,0:T(8,128)(2,1)S(1)} all-gather(bf16[96,128]{1,0:T(8,128)(2,1)S(1)} %get-tuple-element.7), channel_id=1, replica_groups=mesh['outer'=8,'inner'=4] {'outer'}, dimensions={0}, use_global_device_ids=true | all-gather | bytes 221184 | tf_op jit(solution)/shard_map/all_gather | solution.py:130
  144.2 0.0 collective-permute-done.7
  144.2 0.0 collective-permute-start.9
  144.2 0.0 collective-permute-done.8
  144.2 4.7 %collective-permute-start.10 = (bf16[96,128]{1,0:T(8,128)(2,1)S(1)}, bf16[96,128]{1,0:T(8,128)(2,1)S(1)}, u32[]{:S(2)}, u32[]{:S(2)}) collective-permute-start(bf16[96,128]{1,0:T(8,128)(2,1)S(1)} %collective-permute-done.8), channel_id=1, source_target_pairs={{0,28},{4,0},{8,4},{12,8},{16,12},{20,16},{24,20},{28,24},{1,29},{... | collective-permute-start | bytes 73736 | tf_op jit(solution)/shard_map/ppermute | solution.py:25
  149.0 1.8 collective-permute-done.9
  150.7 0.0 collective-permute-start.11
  150.8 0.0 collective-permute-done.10
  150.8 4.7 %collective-permute-start.12 = (bf16[96,128]{1,0:T(8,128)(2,1)S(1)}, bf16[96,128]{1,0:T(8,128)(2,1)S(1)}, u32[]{:S(2)}, u32[]{:S(2)}) collective-permute-start(bf16[96,128]{1,0:T(8,128)(2,1)S(1)} %collective-permute-done.10), channel_id=1, source_target_pairs={{0,28},{4,0},{8,4},{12,8},{16,12},{20,16},{24,20},{28,24},{1,29},{... | collective-permute-start | bytes 73736 | tf_op jit(solution)/shard_map/ppermute | solution.py:25
  155.5 1.8 collective-permute-done.11
  157.3 0.0 collective-permute-start.13
  157.3 0.0 collective-permute-done.12
  157.3 6.5 %collective-permute-done.13 = bf16[96,128]{1,0:T(8,128)(2,1)S(1)} collective-permute-done((bf16[96,128]{1,0:T(8,128)(2,1)S(1)}, bf16[96,128]{1,0:T(8,128)(2,1)S(1)}, u32[]{:S(2)}, u32[]{:S(2)}) %collective-permute-start.13) | collective-permute-done | bytes 24608 | tf_op jit(solution)/shard_map/ppermute | solution.py:22
  163.8 0.3 select_reduce_fusion
  164.1 0.2 fusion.53
  164.4 1.3 convolution_convert_fusion
  165.6 0.0 reduce-scatter.2.cloned.1.call-update
  165.6 17.9 %reduce-scatter.2.cloned.1.call-done = bf16[24,2048]{1,0:T(8,128)(2,1)} async-done(((bf16[96,2048]{1,0:T(8,128)(2,1)}), bf16[24,2048]{1,0:T(8,128)(2,1)}) %reduce-scatter.2.cloned.1.call-update) | async-done | bytes 98320 | tf_op jit(solution)/shard_map/reduce_scatter | solution.py:157
  183.6 0.9 fusion.67
  184.5 1.1 fusion.17
  (23 shorter events, 0.2 us)
Async XLA Ops:
  6.5 157.8 %copy-start = (bf16[128,2048]{1,0:T(8,128)(2,1)S(1)}, bf16[128,2048]{1,0:T(8,128)(2,1)}, u32[]{:S(2)}) copy-start(bf16[128,2048]{1,0:T(8,128)(2,1)} %param.19) | copy-start | bytes 1572868
  6.5 81.7 %all-gather.2.cloned.1.call-start = ((), (), s32[]{:S(2)}) async-start(), calls=%async_computation.1 | async-start | bytes 5242880 | tf_op jit(solution)/shard_map/all_gather | solution.py:94
  7.3 176.3 %reduce-scatter.2.cloned.1.call-start = ((), (), s32[]{:S(2)}) async-start(), calls=%async_computation.2 | async-start | bytes 491520 | tf_op jit(solution)/shard_map/reduce_scatter | solution.py:157
  8.5 20.6 %collective-permute-start.3 = (bf16[192,1024]{0,1:T(8,128)(2,1)S(1)}, bf16[192,1024]{0,1:T(8,128)(2,1)S(1)}, u32[]{:S(2)}, u32[]{:S(2)}) collective-permute-start(bf16[192,1024]{0,1:T(8,128)(2,1)S(1)} %copy.16), channel_id=1, source_target_pairs={{0,3},{1,4},{2,5},{3,6},{4,7},{5,8},{6,9},{7,10},{8,11},{9,12},{10... | collective-permute-start | bytes 1179656 | tf_op jit(solution)/shard_map/ppermute | solution.py:35
  12.9 33.8 %collective-permute-start.4 = (bf16[192,1024]{0,1:T(8,128)(2,1)S(1)}, bf16[192,1024]{0,1:T(8,128)(2,1)}, u32[]{:S(2)}, u32[]{:S(2)}) collective-permute-start(bf16[192,1024]{0,1:T(8,128)(2,1)S(1)} %copy.16), channel_id=1, source_target_pairs={{0,2},{1,3},{2,4},{3,5},{4,6},{5,7},{6,8},{7,9},{8,10},{9,11},{10,... | collective-permute-start | bytes 1179656 | tf_op jit(solution)/shard_map/ppermute | solution.py:35
  17.0 29.6 %collective-permute-start.5 = (bf16[192,1024]{0,1:T(8,128)(2,1)S(1)}, bf16[192,1024]{0,1:T(8,128)(2,1)}, u32[]{:S(2)}, u32[]{:S(2)}) collective-permute-start(bf16[192,1024]{0,1:T(8,128)(2,1)S(1)} %copy.16), channel_id=1, source_target_pairs={{0,1},{1,2},{2,3},{3,4},{4,5},{5,6},{6,7},{7,8},{8,9},{9,10},{10,1... | collective-permute-start | bytes 1179656 | tf_op jit(solution)/shard_map/ppermute | solution.py:35
  21.5 45.5 %collective-permute-start = (bf16[192,1024]{0,1:T(8,128)(2,1)S(1)}, bf16[192,1024]{0,1:T(8,128)(2,1)}, u32[]{:S(2)}, u32[]{:S(2)}) collective-permute-start(bf16[192,1024]{0,1:T(8,128)(2,1)S(1)} %copy.12), channel_id=1, source_target_pairs={{0,3},{1,4},{2,5},{3,6},{4,7},{5,8},{6,9},{7,10},{8,11},{9,12},{10... | collective-permute-start | bytes 1179656 | tf_op jit(solution)/shard_map/ppermute | solution.py:35
  24.8 53.4 %collective-permute-start.1 = (bf16[192,1024]{0,1:T(8,128)(2,1)S(1)}, bf16[192,1024]{0,1:T(8,128)(2,1)}, u32[]{:S(2)}, u32[]{:S(2)}) collective-permute-start(bf16[192,1024]{0,1:T(8,128)(2,1)S(1)} %copy.12), channel_id=1, source_target_pairs={{0,2},{1,3},{2,4},{3,5},{4,6},{5,7},{6,8},{7,9},{8,10},{9,11},{10,... | collective-permute-start | bytes 1179656 | tf_op jit(solution)/shard_map/ppermute | solution.py:35
  29.1 17.6 %copy-start.2 = (bf16[192,1024]{0,1:T(8,128)(2,1)}, bf16[192,1024]{0,1:T(8,128)(2,1)S(1)}, u32[]{:S(2)}) copy-start(bf16[192,1024]{0,1:T(8,128)(2,1)S(1)} %collective-permute-done.3) | copy-start | bytes 1179652
  29.1 49.1 %collective-permute-start.2 = (bf16[192,1024]{0,1:T(8,128)(2,1)S(1)}, bf16[192,1024]{0,1:T(8,128)(2,1)}, u32[]{:S(2)}, u32[]{:S(2)}) collective-permute-start(bf16[192,1024]{0,1:T(8,128)(2,1)S(1)} %copy.12), channel_id=1, source_target_pairs={{0,1},{1,2},{2,3},{3,4},{4,5},{5,6},{6,7},{7,8},{8,9},{9,10},{10,1... | collective-permute-start | bytes 1179656 | tf_op jit(solution)/shard_map/ppermute | solution.py:35
  48.8 32.7 %copy-start.7 = (bf16[192,1024]{1,0:T(8,128)(2,1)S(1)}, bf16[192,1024]{1,0:T(8,128)(2,1)}, u32[]{:S(2)}) copy-start(bf16[192,1024]{1,0:T(8,128)(2,1)} %param.11) | copy-start | bytes 1179652
  85.2 3.0 %copy-start.1 = (bf16[192,2048]{1,0:T(8,128)(2,1)S(1)}, bf16[192,2048]{1,0:T(8,128)(2,1)}, u32[]{:S(2)}) copy-start(bf16[192,2048]{1,0:T(8,128)(2,1)} %param.10) | copy-start | bytes 2359300
  88.2 10.1 %copy-start.3 = (f32[2048]{0:T(1024)S(1)}, f32[2048]{0:T(1024)}, u32[]{:S(2)}) copy-start(f32[2048]{0:T(1024)} %param.15) | copy-start | bytes 24580
  88.2 20.2 %copy-start.4 = (bf16[2048,128]{1,0:T(8,128)(2,1)S(1)}, bf16[2048,128]{1,0:T(8,128)(2,1)}, u32[]{:S(2)}) copy-start(bf16[2048,128]{1,0:T(8,128)(2,1)} %param.18) | copy-start | bytes 1572868
  88.2 20.1 %copy-start.5 = (bf16[2048,128]{1,0:T(8,128)(2,1)S(1)}, bf16[2048,128]{1,0:T(8,128)(2,1)}, u32[]{:S(2)}) copy-start(bf16[2048,128]{1,0:T(8,128)(2,1)} %param.17) | copy-start | bytes 1572868
  88.2 20.1 %copy-start.6 = (bf16[2048,128]{1,0:T(8,128)(2,1)S(1)}, bf16[2048,128]{1,0:T(8,128)(2,1)}, u32[]{:S(2)}) copy-start(bf16[2048,128]{1,0:T(8,128)(2,1)} %param.16) | copy-start | bytes 1572868
  92.1 6.0 %collective-permute-start.6 = (bf16[7,2048]{1,0:T(8,128)(2,1)S(1)}, bf16[7,2048]{1,0:T(8,128)(2,1)S(1)}, u32[]{:S(2)}, u32[]{:S(2)}) collective-permute-start(bf16[7,2048]{1,0:T(8,128)(2,1)S(1)} %slice.24), channel_id=1, source_target_pairs={{0,1},{1,2},{2,3},{3,4},{4,5},{5,6},{6,7},{7,8},{8,9},{9,10},{10,1... | collective-permute-start | bytes 86024 | tf_op jit(solution)/shard_map/ppermute | solution.py:35
  108.8 35.4 %collective-permute-start.7 = (bf16[96,128]{1,0:T(8,128)(2,1)S(1)}, bf16[96,128]{1,0:T(8,128)(2,1)S(1)}, u32[]{:S(2)}, u32[]{:S(2)}) collective-permute-start(bf16[96,128]{1,0:T(8,128)(2,1)S(1)} %get-tuple-element.5), channel_id=1, source_target_pairs={{0,4},{4,8},{8,12},{12,16},{16,20},{20,24},{24,28},{28,0},{1,5},{5... | collective-permute-start | bytes 73736 | tf_op jit(solution)/shard_map/ppermute | solution.py:22
  110.4 33.9 %collective-permute-start.8 = (bf16[96,128]{1,0:T(8,128)(2,1)S(1)}, bf16[96,128]{1,0:T(8,128)(2,1)S(1)}, u32[]{:S(2)}, u32[]{:S(2)}) collective-permute-start(bf16[96,128]{1,0:T(8,128)(2,1)S(1)} %get-tuple-element.5), channel_id=1, source_target_pairs={{0,28},{4,0},{8,4},{12,8},{16,12},{20,16},{24,20},{28,24},{1,29},{... | collective-permute-start | bytes 73736 | tf_op jit(solution)/shard_map/ppermute | solution.py:25
  144.2 6.5 %collective-permute-start.9 = (bf16[96,128]{1,0:T(8,128)(2,1)S(1)}, bf16[96,128]{1,0:T(8,128)(2,1)S(1)}, u32[]{:S(2)}, u32[]{:S(2)}) collective-permute-start(bf16[96,128]{1,0:T(8,128)(2,1)S(1)} %collective-permute-done.7), channel_id=1, source_target_pairs={{0,4},{4,8},{8,12},{12,16},{16,20},{20,24},{24,28},{28,0},{1,5},{5... | collective-permute-start | bytes 73736 | tf_op jit(solution)/shard_map/ppermute | solution.py:22
  144.2 6.5 %collective-permute-start.10 = (bf16[96,128]{1,0:T(8,128)(2,1)S(1)}, bf16[96,128]{1,0:T(8,128)(2,1)S(1)}, u32[]{:S(2)}, u32[]{:S(2)}) collective-permute-start(bf16[96,128]{1,0:T(8,128)(2,1)S(1)} %collective-permute-done.8), channel_id=1, source_target_pairs={{0,28},{4,0},{8,4},{12,8},{16,12},{20,16},{24,20},{28,24},{1,29},{... | collective-permute-start | bytes 73736 | tf_op jit(solution)/shard_map/ppermute | solution.py:25
  150.7 6.5 %collective-permute-start.11 = (bf16[96,128]{1,0:T(8,128)(2,1)S(1)}, bf16[96,128]{1,0:T(8,128)(2,1)S(1)}, u32[]{:S(2)}, u32[]{:S(2)}) collective-permute-start(bf16[96,128]{1,0:T(8,128)(2,1)S(1)} %collective-permute-done.9), channel_id=1, source_target_pairs={{0,4},{4,8},{8,12},{12,16},{16,20},{20,24},{24,28},{28,0},{1,5},{5... | collective-permute-start | bytes 73736 | tf_op jit(solution)/shard_map/ppermute | solution.py:22
  150.8 6.5 %collective-permute-start.12 = (bf16[96,128]{1,0:T(8,128)(2,1)S(1)}, bf16[96,128]{1,0:T(8,128)(2,1)S(1)}, u32[]{:S(2)}, u32[]{:S(2)}) collective-permute-start(bf16[96,128]{1,0:T(8,128)(2,1)S(1)} %collective-permute-done.10), channel_id=1, source_target_pairs={{0,28},{4,0},{8,4},{12,8},{16,12},{20,16},{24,20},{28,24},{1,29},{... | collective-permute-start | bytes 73736 | tf_op jit(solution)/shard_map/ppermute | solution.py:25
  157.3 6.5 %collective-permute-start.13 = (bf16[96,128]{1,0:T(8,128)(2,1)S(1)}, bf16[96,128]{1,0:T(8,128)(2,1)S(1)}, u32[]{:S(2)}, u32[]{:S(2)}) collective-permute-start(bf16[96,128]{1,0:T(8,128)(2,1)S(1)} %collective-permute-done.11), channel_id=1, source_target_pairs={{0,4},{4,8},{8,12},{12,16},{16,20},{20,24},{24,28},{28,0},{1,5},{5... | collective-permute-start | bytes 73736 | tf_op jit(solution)/shard_map/ppermute | solution.py:22
Sparse Core Ops, SparseCore 0:
  8.9 56.0 all-gather.1
  165.8 17.7 reduce-scatter.1
